TPU v7x, 32 devices: a whole 2x2x4 slice. The times are simulated.
32 devices in a mesh: gx: 4 (over y, x), gy: 2 (over core), gz: 4 (over z).
Axes of the slice: x: 2, y: 2, z: 4, core: 2. Of those that a mesh axis runs over, the one named last changes fastest.
Arguments:
- panel: float32 [4, 2, 16, 256, 256], P('gx', 'gy', 'gz'), may hold values from -120 to 120
- tiles: float32 [4, 2, 16, 10, 256, 256], P('gx', 'gy', 'gz'), may hold values from -0.125 to 0.125
- codes: int32 [4, 2, 16, 10], P('gx', 'gy', 'gz'), may hold values from 0 to 26, as said below
Outputs:
- bands: float32 [4, 2, 16, 256, 256], P('gx', 'gy', 'gz')
- factor: float32 [256, 256], replicated
Inputs may be any that keep to these rules, and one draw needn't show every extreme that they name: Slot 0 of every element holds 13, the element itself; the other 9 slots of an element hold distinct codes other than 13.
All inputs are finite; a program needn't handle non-finite values.
Results may differ from a plain program's by a relative error of at most 0.0003.
Values sent between devices are 32-bit elements; how exact they have to be, the bound alone decides.
A program may use at most 128 MiB of HBM per device.

v0:
```python
import jax
import jax.numpy as jnp
from jax import lax
from jax.sharding import PartitionSpec as P


def padded_2(shard, sides, width):
    for axis, dim in sides:
        peers, length = (lax.axis_size(axis), shard.shape[dim])
        up = [(i, (i + 1) % peers) for i in range(peers - 1)]
        down = [(j, i) for i, j in up]
        last = lax.slice_in_dim(shard, length - width, length, axis=dim)
        initial = lax.slice_in_dim(shard, 0, width, axis=dim)
        before = lax.ppermute(last, axis, up)
        after = lax.ppermute(initial, axis, down)
        shard = jnp.concatenate([before, shard, after], axis=dim)
    return shard


def window(padded, first, second, third):
    zero = jnp.zeros((), jnp.int32)
    piece = lax.dynamic_slice(
        padded, (first, second, third, zero, zero), (1, 1, 1, padded.shape[3], padded.shape[4])
    )
    return piece[0, 0, 0]


def per_device(panel, tiles, codes):
    along_x = padded_2(panel, (("gx", 0),), 1)
    along_y = padded_2(along_x, (("gy", 1),), 1)
    padded = padded_2(along_y, (("gz", 2),), 1)
    width = panel.shape[4]
    products = []
    for element_cell in range(panel.shape[2]):
        slot_codes = codes[0, 0, element_cell]
        windows = jax.vmap(lambda c: window(padded, c // 9, c // 3 % 3, element_cell + c % 3))(
            slot_codes
        )
        applied = jnp.einsum(
            "kab,kbc->ac", tiles[0, 0, element_cell], windows, precision=lax.Precision.HIGHEST
        )
        products.append(applied - 0.5 * panel[0, 0, element_cell])
    filtered = jnp.stack(products)
    flat_rows = filtered.reshape(-1, width)
    local_gram = jnp.dot(flat_rows.T, flat_rows, precision=lax.Precision.HIGHEST)
    row_total = flat_rows.shape[0] * lax.axis_size("gx") * lax.axis_size("gy") * lax.axis_size("gz")
    gram_part = lax.psum_scatter(local_gram, "gz", scatter_dimension=0, tiled=True)
    gram_part = lax.psum(gram_part, ("gx", "gy"))
    summed = lax.all_gather(gram_part, "gz", axis=0, tiled=True)
    gram = summed / row_total
    lower = jnp.linalg.cholesky(gram)
    inverse = lax.linalg.triangular_solve(
        lower, jnp.eye(width, dtype=gram.dtype), left_side=True, lower=True
    )
    bands = jnp.dot(flat_rows, inverse.T, precision=lax.Precision.HIGHEST).reshape(panel.shape)
    return (bands, lower.T)


def solution(mesh):
    in_specs = (
        P("gx", "gy", "gz", None, None),
        P("gx", "gy", "gz", None, None, None),
        P("gx", "gy", "gz", None),
    )
    out_specs = (P("gx", "gy", "gz", None, None), P())
    return jax.shard_map(
        per_device, mesh=mesh, in_specs=in_specs, out_specs=out_specs, check_vma=False
    )
```

profile of v0, /device:TPU:0, one launch (start us, length us, event | category | flops | bytes accessed | tf_op | source)
XLA Modules:
  0.0 357.0 jit_solution(12483435723269355721)
XLA Ops:
  7.2 5.1 %collective-permute-start = (f32[1,1,4,256,256]{4,3,2,1,0:T(8,128)}, f32[1,1,4,256,256]{4,3,2,1,0:T(8,128)S(1)}, u32[]{:S(2)}, u32[]{:S(2)}) collective-permute-start(f32[1,1,4,256,256]{4,3,2,1,0:T(8,128)} %param.3), channel_id=1, source_target_pairs={{0,8},{8,16},{16,24},{1,9},{9,17},{17,25},{2,10},{10,18},{18,26},{... | collective-permute-start | bytes 3145736 | tf_op jit(solution)/shard_map/ppermute | solution.py:14
  13.6 21.3 %collective-permute-done = f32[1,1,4,256,256]{4,3,2,1,0:T(8,128)S(1)} collective-permute-done((f32[1,1,4,256,256]{4,3,2,1,0:T(8,128)}, f32[1,1,4,256,256]{4,3,2,1,0:T(8,128)S(1)}, u32[]{:S(2)}, u32[]{:S(2)}) %collective-permute-start) | collective-permute-done | bytes 1048608 | tf_op jit(solution)/shard_map/ppermute | solution.py:14
  35.1 24.1 %collective-permute-done.1 = f32[1,1,4,256,256]{4,3,2,1,0:T(8,128)S(1)} collective-permute-done((f32[1,1,4,256,256]{4,3,2,1,0:T(8,128)}, f32[1,1,4,256,256]{4,3,2,1,0:T(8,128)S(1)}, u32[]{:S(2)}, u32[]{:S(2)}) %collective-permute-start.1) | collective-permute-done | bytes 1048608 | tf_op jit(solution)/shard_map/ppermute | solution.py:15
  59.3 1.5 collective-permute-start.2
  62.1 3.8 %collective-permute-done.2 = f32[3,1,4,256,256]{4,3,2,1,0:T(8,128)S(1)} collective-permute-done((f32[3,1,4,256,256]{4,3,2,1,0:T(8,128)S(1)}, f32[3,1,4,256,256]{4,3,2,1,0:T(8,128)S(1)}, u32[]{:S(2)}, u32[]{:S(2)}) %collective-permute-start.2) | collective-permute-done | bytes 3145760 | tf_op jit(solution)/shard_map/ppermute | solution.py:14
  65.9 2.5 collective-permute-done.3
  68.4 2.8 pad_maximum_fusion.3
  71.4 5.0 %collective-permute-start.4 = (f32[3,3,1,256,256]{4,3,2,1,0:T(8,128)}, f32[3,3,1,256,256]{4,3,2,1,0:T(8,128)}, u32[]{:S(2)}, u32[]{:S(2)}) collective-permute-start(f32[3,3,1,256,256]{4,3,2,1,0:T(8,128)} %get-tuple-element.24), channel_id=1, source_target_pairs={{0,1},{1,2},{2,3},{4,5},{5,6},{6,7},{8,9},{9,10},{10,11},{12,13},{... | collective-permute-start | bytes 7077896 | tf_op jit(solution)/shard_map/ppermute | solution.py:14
  80.6 1.8 copy.44
  82.4 1.8 copy.43
  84.2 41.9 %collective-permute-done.4 = f32[3,3,1,256,256]{4,3,2,1,0:T(8,128)} collective-permute-done((f32[3,3,1,256,256]{4,3,2,1,0:T(8,128)}, f32[3,3,1,256,256]{4,3,2,1,0:T(8,128)}, u32[]{:S(2)}, u32[]{:S(2)}) %collective-permute-start.4) | collective-permute-done | bytes 2359328 | tf_op jit(solution)/shard_map/ppermute | solution.py:14
  126.1 5.5 %collective-permute-done.5 = f32[3,3,1,256,256]{4,3,2,1,0:T(8,128)} collective-permute-done((f32[3,3,1,256,256]{4,3,2,1,0:T(8,128)}, f32[3,3,1,256,256]{4,3,2,1,0:T(8,128)}, u32[]{:S(2)}, u32[]{:S(2)}) %collective-permute-start.5) | collective-permute-done | bytes 2359328 | tf_op jit(solution)/shard_map/ppermute | solution.py:15
  131.7 9.7 %pad_maximum_fusion = f32[3,3,6,256,256]{4,3,2,1,0:T(8,128)} fusion(f32[3,3,1,256,256]{4,3,2,1,0:T(8,128)} %collective-permute-done.5, f32[3,1,4,256,256]{4,3,2,1,0:T(8,128)} %copy-done.1, f32[3,1,4,256,256]{4,3,2,1,0:T(8,128)S(1)} %constant_dynamic-update-slice_fusion, f32[3,1,4,256,256]{4,3,2,1,0:T(8,128)} %copy-done, ...), kind=kLoop, calls=%fused_computation.6 | loop fusion | flops 14155776 | bytes 28311552 | tf_op jit(solution)/shard_map/concatenate | solution.py:16
  141.3 7.3 %gather_fusion.3 = f32[10,256,256]{2,1,0:T(8,128)} fusion(f32[3,3,6,256,256]{4,3,2,1,0:T(8,128)} %pad_maximum_fusion, s32[10]{0:T(128)S(1)} %get-tuple-element.38), kind=kCustom, calls=%fused_computation.3 | custom fusion | bytes 5243080 | tf_op jit(solution)/shard_map/vmap()/gather | solution.py:22
  148.6 7.4 %gather_fusion.2 = f32[10,256,256]{2,1,0:T(8,128)} fusion(f32[3,3,6,256,256]{4,3,2,1,0:T(8,128)} %pad_maximum_fusion, s32[10]{0:T(128)S(1)} %get-tuple-element.39), kind=kCustom, calls=%fused_computation.2 | custom fusion | bytes 5243080 | tf_op jit(solution)/shard_map/vmap()/gather | solution.py:22
  156.0 5.7 %gather_fusion.1 = f32[10,256,256]{2,1,0:T(8,128)S(1)} fusion(f32[3,3,6,256,256]{4,3,2,1,0:T(8,128)} %pad_maximum_fusion, s32[10]{0:T(128)S(1)} %get-tuple-element.37), kind=kCustom, calls=%fused_computation.1 | custom fusion | bytes 5243080 | tf_op jit(solution)/shard_map/vmap()/gather | solution.py:22
  161.8 7.4 %gather_fusion = f32[10,256,256]{2,1,0:T(8,128)} fusion(f32[3,3,6,256,256]{4,3,2,1,0:T(8,128)} %pad_maximum_fusion, s32[10]{0:T(128)S(1)} %get-tuple-element.36), kind=kCustom, calls=%fused_computation | custom fusion | bytes 5243080 | tf_op jit(solution)/shard_map/vmap()/gather | solution.py:22
  169.2 7.0 %fusion.27 = f32[1,256,256]{1,2,0:T(8,128)S(1)} fusion(f32[10,256,256]{2,1,0:T(8,128)} %gather_fusion.3, f32[1,1,4,10,256,256]{5,4,3,2,1,0:T(8,128)} %param.4, f32[1,1,1,256,256]{3,4,2,1,0:T(8,128)S(1)} %copy-done.7), kind=kOutput, calls=%fused_computation.29 | convolution fusion | flops 2013396992 | bytes 5767168 | tf_op jit(solution)/shard_map/kab,kbc->ac/dot_general | solution.py:39
  176.1 6.2 %fusion.33 = f32[1,256,256]{1,2,0:T(8,128)S(1)} fusion(f32[10,256,256]{2,1,0:T(8,128)S(1)} %copy-done.3, f32[1,1,4,10,256,256]{5,4,3,2,1,0:T(8,128)} %param.4, f32[1,1,1,256,256]{3,4,2,1,0:T(8,128)S(1)} %copy.45), kind=kOutput, calls=%fused_computation.31 | convolution fusion | flops 2013396992 | bytes 5767168 | tf_op jit(solution)/shard_map/kab,kbc->ac/dot_general | solution.py:39
  182.4 6.7 %fusion.39 = f32[1,256,256]{1,2,0:T(8,128)S(1)} fusion(f32[10,256,256]{2,1,0:T(8,128)S(1)} %gather_fusion.1, f32[1,1,4,10,256,256]{5,4,3,2,1,0:T(8,128)} %param.4, f32[1,1,1,256,256]{3,4,2,1,0:T(8,128)S(1)} %copy-done.5), kind=kOutput, calls=%fused_computation.33 | convolution fusion | flops 2013396992 | bytes 5767168 | tf_op jit(solution)/shard_map/kab,kbc->ac/dot_general | solution.py:39
  189.1 6.2 %fusion.45 = f32[1,256,256]{1,2,0:T(8,128)S(1)} fusion(f32[10,256,256]{2,1,0:T(8,128)S(1)} %copy-done.2, f32[1,1,4,10,256,256]{5,4,3,2,1,0:T(8,128)} %param.4, f32[1,1,1,256,256]{3,4,2,1,0:T(8,128)S(1)} %copy-done.6), kind=kOutput, calls=%fused_computation.35 | convolution fusion | flops 2013396992 | bytes 5767168 | tf_op jit(solution)/shard_map/kab,kbc->ac/dot_general | solution.py:39
  195.4 1.7 convolution_bitcast_fusion.1
  197.2 18.0 %reduce-scatter.4.cloned.1.call-done = f32[64,256]{1,0:T(8,128)} async-done(((f32[256,256]{1,0:T(8,128)}), f32[64,256]{1,0:T(8,128)}) %reduce-scatter.4.cloned.1.call-update) | async-done | bytes 65552
  215.2 1.6 copy.42
  216.8 53.7 %all-reduce.3.cloned.1.call-done = f32[64,256]{0,1:T(8,128)} async-done(((f32[64,256]{0,1:T(8,128)}), f32[64,256]{0,1:T(8,128)}) %all-reduce.3.cloned.1.call-update) | async-done | bytes 65552 | tf_op jit(solution)/shard_map/psum | solution.py:48
  271.5 14.1 %all_gather.3 = f32[256,256]{1,0:T(8,128)S(1)} all-gather(f32[64,256]{1,0:T(8,128)S(1)} %copy.28), channel_id=1, replica_groups=mesh['gx'=4,'gy'=2,'gz'=4] {'gz'}, dimensions={0}, use_global_device_ids=true | all-gather | bytes 327680 | tf_op jit(solution)/shard_map/all_gather | solution.py:49
  285.9 11.7 %cholesky.50 = f32[128,128]{1,0:T(8,128)S(1)} custom-call(f32[128,128]{1,0:T(8,128)S(1)} %cholesky.118), custom_call_target="Cholesky" | custom-call | tf_op jit(solution)/shard_map/jit(cholesky)/cholesky | solution.py:51
  297.7 9.8 %custom-call.14 = f32[1,128,128]{1,2,0:T(8,128)S(1)} custom-call(f32[1,128,128]{2,1,0:T(8,128)S(1)} %get-tuple-element.35), custom_call_target="InvertDiagBlocksLowerTriangular" | custom-call | tf_op jit(solution)/shard_map/jit(cholesky)/cholesky | solution.py:51
  308.0 11.7 %cholesky.105 = f32[128,128]{1,0:T(8,128)S(1)} custom-call(f32[128,128]{1,0:T(8,128)S(1)} %convolution_subtract_fusion.1), custom_call_target="Cholesky" | custom-call | tf_op jit(solution)/shard_map/jit(cholesky)/cholesky | solution.py:51
  321.7 4.0 %while.1 = (s32[]{:T(128)}, f32[256,256]{1,0:T(8,128)S(1)}, s32[2,2]{1,0:T(2,128)S(1)}, f32[2,128,128]{2,1,0:T(8,128)S(1)}, s32[]{:T(128)}) while((s32[]{:T(128)}, f32[256,256]{1,0:T(8,128)S(1)}, s32[2,2]{1,0:T(2,128)S(1)}, f32[2,128,128]{2,1,0:T(8,128)S(1)}, s32[]{:T(128)}) %tuple.37), condition=%wide.while_cond, body=%wide.while_body.sunk | while | flops 2 | bytes 131181 | solution.py:52
  325.7 19.7 %custom-call.15 = f32[2,128,128]{1,2,0:T(8,128)S(1)} custom-call(f32[2,128,128]{2,1,0:T(8,128)S(1)} %get-tuple-element.9), custom_call_target="InvertDiagBlocksLowerTriangular" | custom-call | tf_op jit(solution)/shard_map/triangular_solve | solution.py:52
  346.3 2.8 convolution_bitcast_fusion
  (59 shorter events, 15.5 us)
Async XLA Ops:
  7.2 208.0 %reduce-scatter.4.cloned.1.call-start = ((), (), s32[]{:S(2)}) async-start(), calls=%async_computation.2 | async-start | bytes 327680
  7.2 27.8 %copy-start.4 = (f32[1,1,4,256,256]{4,3,2,1,0:T(8,128)S(1)}, f32[1,1,4,256,256]{4,3,2,1,0:T(8,128)}, u32[]{:S(2)}) copy-start(f32[1,1,4,256,256]{4,3,2,1,0:T(8,128)} %param.3) | copy-start | bytes 3145732
  7.2 27.7 %collective-permute-start = (f32[1,1,4,256,256]{4,3,2,1,0:T(8,128)}, f32[1,1,4,256,256]{4,3,2,1,0:T(8,128)S(1)}, u32[]{:S(2)}, u32[]{:S(2)}) collective-permute-start(f32[1,1,4,256,256]{4,3,2,1,0:T(8,128)} %param.3), channel_id=1, source_target_pairs={{0,8},{8,16},{16,24},{1,9},{9,17},{17,25},{2,10},{10,18},{18,26},{... | collective-permute-start | bytes 3145736 | tf_op jit(solution)/shard_map/ppermute | solution.py:14
  12.3 47.0 %collective-permute-start.1 = (f32[1,1,4,256,256]{4,3,2,1,0:T(8,128)}, f32[1,1,4,256,256]{4,3,2,1,0:T(8,128)S(1)}, u32[]{:S(2)}, u32[]{:S(2)}) collective-permute-start(f32[1,1,4,256,256]{4,3,2,1,0:T(8,128)} %param.3), channel_id=1, source_target_pairs={{8,0},{16,8},{24,16},{9,1},{17,9},{25,17},{10,2},{18,10},{26,18},{... | collective-permute-start | bytes 3145736 | tf_op jit(solution)/shard_map/ppermute | solution.py:15
  59.3 6.6 %collective-permute-start.2 = (f32[3,1,4,256,256]{4,3,2,1,0:T(8,128)S(1)}, f32[3,1,4,256,256]{4,3,2,1,0:T(8,128)S(1)}, u32[]{:S(2)}, u32[]{:S(2)}) collective-permute-start(f32[3,1,4,256,256]{4,3,2,1,0:T(8,128)S(1)} %constant_dynamic-update-slice_fusion), channel_id=1, source_target_pairs={{0,4},{1,5},{2,6},{3,7},{8,12},{9,13},{10,14},{11,15},{16,20},{17,... | collective-permute-start | bytes 9437192 | tf_op jit(solution)/shard_map/ppermute | solution.py:14
  60.8 7.6 %collective-permute-start.3 = (f32[3,1,4,256,256]{4,3,2,1,0:T(8,128)S(1)}, f32[3,1,4,256,256]{4,3,2,1,0:T(8,128)S(1)}, u32[]{:S(2)}, u32[]{:S(2)}) collective-permute-start(f32[3,1,4,256,256]{4,3,2,1,0:T(8,128)S(1)} %constant_dynamic-update-slice_fusion), channel_id=1, source_target_pairs={{4,0},{5,1},{6,2},{7,3},{12,8},{13,9},{14,10},{15,11},{20,16},{21,... | collective-permute-start | bytes 9437192 | tf_op jit(solution)/shard_map/ppermute | solution.py:15
  65.9 5.3 %copy-start = (f32[3,1,4,256,256]{4,3,2,1,0:T(8,128)}, f32[3,1,4,256,256]{4,3,2,1,0:T(8,128)S(1)}, u32[]{:S(2)}) copy-start(f32[3,1,4,256,256]{4,3,2,1,0:T(8,128)S(1)} %collective-permute-done.2) | copy-start | bytes 9437188
  68.4 3.0 copy-start.1
  71.4 12.8 %copy-start.8 = (s32[1,1,4,10]{3,2,1,0:T(4,128)S(1)}, s32[1,1,4,10]{3,2,1,0:T(4,128)}, u32[]{:S(2)}) copy-start(s32[1,1,4,10]{3,2,1,0:T(4,128)} %param.5) | copy-start | bytes 484
  71.4 54.7 %collective-permute-start.4 = (f32[3,3,1,256,256]{4,3,2,1,0:T(8,128)}, f32[3,3,1,256,256]{4,3,2,1,0:T(8,128)}, u32[]{:S(2)}, u32[]{:S(2)}) collective-permute-start(f32[3,3,1,256,256]{4,3,2,1,0:T(8,128)} %get-tuple-element.24), channel_id=1, source_target_pairs={{0,1},{1,2},{2,3},{4,5},{5,6},{6,7},{8,9},{9,10},{10,11},{12,13},{... | collective-permute-start | bytes 7077896 | tf_op jit(solution)/shard_map/ppermute | solution.py:14
  76.4 55.2 %collective-permute-start.5 = (f32[3,3,1,256,256]{4,3,2,1,0:T(8,128)}, f32[3,3,1,256,256]{4,3,2,1,0:T(8,128)}, u32[]{:S(2)}, u32[]{:S(2)}) collective-permute-start(f32[3,3,1,256,256]{4,3,2,1,0:T(8,128)} %get-tuple-element.25), channel_id=1, source_target_pairs={{1,0},{2,1},{3,2},{5,4},{6,5},{7,6},{9,8},{10,9},{11,10},{13,12},{... | collective-permute-start | bytes 7077896 | tf_op jit(solution)/shard_map/ppermute | solution.py:15
  161.7 7.4 %copy-start.7 = (f32[1,1,1,256,256]{3,4,2,1,0:T(8,128)S(1)}, f32[1,1,1,256,256]{3,4,2,1,0:T(8,128)}, u32[]{:S(2)}) copy-start(f32[1,1,1,256,256]{3,4,2,1,0:T(8,128)} %copy.46) | copy-start | bytes 786436
  169.2 7.0 %copy-start.3 = (f32[10,256,256]{2,1,0:T(8,128)S(1)}, f32[10,256,256]{2,1,0:T(8,128)}, u32[]{:S(2)}) copy-start(f32[10,256,256]{2,1,0:T(8,128)} %gather_fusion.2) | copy-start | bytes 7864324
  176.1 6.3 %copy-start.5 = (f32[1,1,1,256,256]{3,4,2,1,0:T(8,128)S(1)}, f32[1,1,1,256,256]{3,4,2,1,0:T(8,128)}, u32[]{:S(2)}) copy-start(f32[1,1,1,256,256]{3,4,2,1,0:T(8,128)} %copy.44) | copy-start | bytes 786436
  182.4 6.7 %copy-start.2 = (f32[10,256,256]{2,1,0:T(8,128)S(1)}, f32[10,256,256]{2,1,0:T(8,128)}, u32[]{:S(2)}) copy-start(f32[10,256,256]{2,1,0:T(8,128)} %gather_fusion) | copy-start | bytes 7864324
  182.4 6.7 %copy-start.6 = (f32[1,1,1,256,256]{3,4,2,1,0:T(8,128)S(1)}, f32[1,1,1,256,256]{3,4,2,1,0:T(8,128)}, u32[]{:S(2)}) copy-start(f32[1,1,1,256,256]{3,4,2,1,0:T(8,128)} %copy.43) | copy-start | bytes 786436
  197.1 73.4 %all-reduce.3.cloned.1.call-start = ((), (), s32[]{:S(2)}) async-start(), calls=%async_computation.1 | async-start | bytes 262144 | tf_op jit(solution)/shard_map/psum | solution.py:48
Sparse Core Ops, SparseCore 0:
  197.2 17.8 reduce-scatter.3
  218.8 51.6 all-reduce.2
where the time goes:
time: 360 us; the launch traced here: 357 us
  waiting for transfers between devices  171 us (48%)
  other arithmetic  66.3 us (18%)
  local copies, waits for them, and re-layouts  42.3 us (12%)
  matrix products  31.9 us (9%)
  between operations  15.8 us (4%)
  starting transfers between devices  15.5 us (4%)
  blocking collectives  14.1 us (4%)
    ppermute x3, waiting for transfers between devices, padded_2(): before = lax.ppermute(last, axis, up)  67 us
    psum x1, waiting for transfers between devices, per_device(): gram_part = lax.psum(gram_part, ('gx', 'gy'))  53.7 us
    another operation x6, other arithmetic, per_device(): lower = jnp.linalg.cholesky(gram)  34 us
    ppermute x3, waiting for transfers between devices, padded_2(): after = lax.ppermute(initial, axis, down)  32.1 us
    gather x4, local copies, waits for them, and re-layouts, window(): lax.dynamic_slice(padded, (first, second, third, zero, zero), (1, 1, 1, p...  27.8 us
    dot_general x4, matrix products, per_device(): jnp.einsum('kab,kbc->ac', tiles[0, 0, element_cell], windows, precision=l...  26.1 us
    another operation x2, other arithmetic, per_device(): lax.linalg.triangular_solve(lower, jnp.eye(width, dtype=gram.dtype), left...  19.7 us
    unnamed x3, waiting for transfers between devices  18 us
  transfers between devices with their start and end apart: 8, of which 8 were waited for; matrix products, arithmetic and copies ran while one was open for 2% of the time, Pallas kernels for 0%

commit v1 on v0

--- a/solution.py
+++ b/solution.py
@@ -45,7 +45,7 @@
     local_gram = jnp.dot(flat_rows.T, flat_rows, precision=lax.Precision.HIGHEST)
     row_total = flat_rows.shape[0] * lax.axis_size("gx") * lax.axis_size("gy") * lax.axis_size("gz")
     gram_part = lax.psum_scatter(local_gram, "gz", scatter_dimension=0, tiled=True)
-    gram_part = lax.psum(gram_part, ("gx", "gy"))
+    gram_part = jnp.sum(lax.all_gather(gram_part, axis_name=("gx", "gy")), axis=0)
     summed = lax.all_gather(gram_part, "gz", axis=0, tiled=True)
     gram = summed / row_total
     lower = jnp.linalg.cholesky(gram)

time: 360 us -> 315 us (0.88)
  waiting for transfers between devices: 171 us -> 117 us
  blocking collectives: 14.1 us -> 24.8 us
    psum x1 -> x0, waiting for transfers between devices: 53.7 us -> none  [per_device(): gram_part = lax.psum(gram_part, ('gx', 'gy'))]
    unnamed x3 -> x1, waiting for transfers between devices: 18 us -> 0.02 us
    reduce_scatter x0 -> x1, waiting for transfers between devices: none -> 18 us  [per_device(): lax.psum_scatter(local_gram, 'gz', scatter_dimension=0, tiled=True)]
    all_gather x0 -> x1, blocking collectives: none -> 10.1 us  [per_device(): lax.all_gather(gram_part, axis_name=('gx', 'gy'))]
    unnamed x26 -> x25, local copies, waits for them, and re-layouts: 8.34 us -> 6.75 us
  transfers between devices with their start and end apart: 8 -> 7, of which waited for: 8 -> 7; matrix products, arithmetic and copies ran while one was open for 2% -> 2% of each run, Pallas kernels for 0% -> 0%
where the time goes in v1:
time: 315 us; the launch traced here: 312 us
  waiting for transfers between devices  117 us (37%)
  other arithmetic  66.4 us (21%)
  local copies, waits for them, and re-layouts  39.9 us (13%)
  matrix products  31.9 us (10%)
  blocking collectives  24.8 us (8%)
  between operations  15.9 us (5%)
  starting transfers between devices  15.5 us (5%)
    ppermute x3, waiting for transfers between devices, padded_2(): before = lax.ppermute(last, axis, up)  67 us
    another operation x6, other arithmetic, per_device(): lower = jnp.linalg.cholesky(gram)  34 us
    ppermute x3, waiting for transfers between devices, padded_2(): after = lax.ppermute(initial, axis, down)  32.1 us
    gather x4, local copies, waits for them, and re-layouts, window(): lax.dynamic_slice(padded, (first, second, third, zero, zero), (1, 1, 1, p...  27.8 us
    dot_general x4, matrix products, per_device(): jnp.einsum('kab,kbc->ac', tiles[0, 0, element_cell], windows, precision=l...  26.1 us
    another operation x2, other arithmetic, per_device(): lax.linalg.triangular_solve(lower, jnp.eye(width, dtype=gram.dtype), left...  19.7 us
    reduce_scatter x1, waiting for transfers between devices, per_device(): lax.psum_scatter(local_gram, 'gz', scatter_dimension=0, tiled=True)  18 us
    all_gather x1, blocking collectives, per_device(): summed = lax.all_gather(gram_part, 'gz', axis=0, tiled=True)  14.7 us
  transfers between devices with their start and end apart: 7, of which 7 were waited for; matrix products, arithmetic and copies ran while one was open for 2% of the time, Pallas kernels for 0%

profile of v1, /device:TPU:0, one launch (start us, length us, event | category | flops | bytes accessed | tf_op | source)
XLA Modules:
  0.0 311.7 jit_solution(11853047440970672563)
XLA Ops:
  7.2 5.1 %collective-permute-start = (f32[1,1,4,256,256]{4,3,2,1,0:T(8,128)}, f32[1,1,4,256,256]{4,3,2,1,0:T(8,128)S(1)}, u32[]{:S(2)}, u32[]{:S(2)}) collective-permute-start(f32[1,1,4,256,256]{4,3,2,1,0:T(8,128)} %param.3), channel_id=1, source_target_pairs={{0,8},{8,16},{16,24},{1,9},{9,17},{17,25},{2,10},{10,18},{18,26},{... | collective-permute-start | bytes 3145736 | tf_op jit(solution)/shard_map/ppermute | solution.py:14
  13.6 21.3 %collective-permute-done = f32[1,1,4,256,256]{4,3,2,1,0:T(8,128)S(1)} collective-permute-done((f32[1,1,4,256,256]{4,3,2,1,0:T(8,128)}, f32[1,1,4,256,256]{4,3,2,1,0:T(8,128)S(1)}, u32[]{:S(2)}, u32[]{:S(2)}) %collective-permute-start) | collective-permute-done | bytes 1048608 | tf_op jit(solution)/shard_map/ppermute | solution.py:14
  35.1 24.1 %collective-permute-done.1 = f32[1,1,4,256,256]{4,3,2,1,0:T(8,128)S(1)} collective-permute-done((f32[1,1,4,256,256]{4,3,2,1,0:T(8,128)}, f32[1,1,4,256,256]{4,3,2,1,0:T(8,128)S(1)}, u32[]{:S(2)}, u32[]{:S(2)}) %collective-permute-start.1) | collective-permute-done | bytes 1048608 | tf_op jit(solution)/shard_map/ppermute | solution.py:15
  59.3 1.5 collective-permute-start.2
  62.1 3.8 %collective-permute-done.2 = f32[3,1,4,256,256]{4,3,2,1,0:T(8,128)S(1)} collective-permute-done((f32[3,1,4,256,256]{4,3,2,1,0:T(8,128)S(1)}, f32[3,1,4,256,256]{4,3,2,1,0:T(8,128)S(1)}, u32[]{:S(2)}, u32[]{:S(2)}) %collective-permute-start.2) | collective-permute-done | bytes 3145760 | tf_op jit(solution)/shard_map/ppermute | solution.py:14
  65.9 2.5 collective-permute-done.3
  68.4 2.8 pad_maximum_fusion.3
  71.4 5.0 %collective-permute-start.4 = (f32[3,3,1,256,256]{4,3,2,1,0:T(8,128)}, f32[3,3,1,256,256]{4,3,2,1,0:T(8,128)}, u32[]{:S(2)}, u32[]{:S(2)}) collective-permute-start(f32[3,3,1,256,256]{4,3,2,1,0:T(8,128)} %get-tuple-element.24), channel_id=1, source_target_pairs={{0,1},{1,2},{2,3},{4,5},{5,6},{6,7},{8,9},{9,10},{10,11},{12,13},{... | collective-permute-start | bytes 7077896 | tf_op jit(solution)/shard_map/ppermute | solution.py:14
  80.6 1.8 copy.37
  82.4 1.8 copy.36
  84.3 41.9 %collective-permute-done.4 = f32[3,3,1,256,256]{4,3,2,1,0:T(8,128)} collective-permute-done((f32[3,3,1,256,256]{4,3,2,1,0:T(8,128)}, f32[3,3,1,256,256]{4,3,2,1,0:T(8,128)}, u32[]{:S(2)}, u32[]{:S(2)}) %collective-permute-start.4) | collective-permute-done | bytes 2359328 | tf_op jit(solution)/shard_map/ppermute | solution.py:14
  126.1 5.5 %collective-permute-done.5 = f32[3,3,1,256,256]{4,3,2,1,0:T(8,128)} collective-permute-done((f32[3,3,1,256,256]{4,3,2,1,0:T(8,128)}, f32[3,3,1,256,256]{4,3,2,1,0:T(8,128)}, u32[]{:S(2)}, u32[]{:S(2)}) %collective-permute-start.5) | collective-permute-done | bytes 2359328 | tf_op jit(solution)/shard_map/ppermute | solution.py:15
  131.7 9.7 %pad_maximum_fusion = f32[3,3,6,256,256]{4,3,2,1,0:T(8,128)} fusion(f32[3,3,1,256,256]{4,3,2,1,0:T(8,128)} %collective-permute-done.5, f32[3,1,4,256,256]{4,3,2,1,0:T(8,128)} %copy-done.1, f32[3,1,4,256,256]{4,3,2,1,0:T(8,128)S(1)} %constant_dynamic-update-slice_fusion, f32[3,1,4,256,256]{4,3,2,1,0:T(8,128)} %copy-done, ...), kind=kLoop, calls=%fused_computation.6 | loop fusion | flops 14155776 | bytes 28311552 | tf_op jit(solution)/shard_map/concatenate | solution.py:16
  141.4 7.3 %gather_fusion.3 = f32[10,256,256]{2,1,0:T(8,128)} fusion(f32[3,3,6,256,256]{4,3,2,1,0:T(8,128)} %pad_maximum_fusion, s32[10]{0:T(128)S(1)} %get-tuple-element.38), kind=kCustom, calls=%fused_computation.3 | custom fusion | bytes 5243080 | tf_op jit(solution)/shard_map/vmap()/gather | solution.py:22
  148.7 7.4 %gather_fusion.2 = f32[10,256,256]{2,1,0:T(8,128)} fusion(f32[3,3,6,256,256]{4,3,2,1,0:T(8,128)} %pad_maximum_fusion, s32[10]{0:T(128)S(1)} %get-tuple-element.39), kind=kCustom, calls=%fused_computation.2 | custom fusion | bytes 5243080 | tf_op jit(solution)/shard_map/vmap()/gather | solution.py:22
  156.0 5.7 %gather_fusion.1 = f32[10,256,256]{2,1,0:T(8,128)S(1)} fusion(f32[3,3,6,256,256]{4,3,2,1,0:T(8,128)} %pad_maximum_fusion, s32[10]{0:T(128)S(1)} %get-tuple-element.37), kind=kCustom, calls=%fused_computation.1 | custom fusion | bytes 5243080 | tf_op jit(solution)/shard_map/vmap()/gather | solution.py:22
  161.8 7.4 %gather_fusion = f32[10,256,256]{2,1,0:T(8,128)} fusion(f32[3,3,6,256,256]{4,3,2,1,0:T(8,128)} %pad_maximum_fusion, s32[10]{0:T(128)S(1)} %get-tuple-element.36), kind=kCustom, calls=%fused_computation | custom fusion | bytes 5243080 | tf_op jit(solution)/shard_map/vmap()/gather | solution.py:22
  169.2 7.0 %fusion.27 = f32[1,256,256]{1,2,0:T(8,128)S(1)} fusion(f32[10,256,256]{2,1,0:T(8,128)} %gather_fusion.3, f32[1,1,4,10,256,256]{5,4,3,2,1,0:T(8,128)} %param.4, f32[1,1,1,256,256]{3,4,2,1,0:T(8,128)S(1)} %copy-done.7), kind=kOutput, calls=%fused_computation.29 | convolution fusion | flops 2013396992 | bytes 5767168 | tf_op jit(solution)/shard_map/kab,kbc->ac/dot_general | solution.py:39
  176.2 6.2 %fusion.33 = f32[1,256,256]{1,2,0:T(8,128)S(1)} fusion(f32[10,256,256]{2,1,0:T(8,128)S(1)} %copy-done.3, f32[1,1,4,10,256,256]{5,4,3,2,1,0:T(8,128)} %param.4, f32[1,1,1,256,256]{3,4,2,1,0:T(8,128)S(1)} %copy.38), kind=kOutput, calls=%fused_computation.31 | convolution fusion | flops 2013396992 | bytes 5767168 | tf_op jit(solution)/shard_map/kab,kbc->ac/dot_general | solution.py:39
  182.5 6.7 %fusion.39 = f32[1,256,256]{1,2,0:T(8,128)S(1)} fusion(f32[10,256,256]{2,1,0:T(8,128)S(1)} %gather_fusion.1, f32[1,1,4,10,256,256]{5,4,3,2,1,0:T(8,128)} %param.4, f32[1,1,1,256,256]{3,4,2,1,0:T(8,128)S(1)} %copy-done.5), kind=kOutput, calls=%fused_computation.33 | convolution fusion | flops 2013396992 | bytes 5767168 | tf_op jit(solution)/shard_map/kab,kbc->ac/dot_general | solution.py:39
  189.2 6.2 %fusion.45 = f32[1,256,256]{1,2,0:T(8,128)S(1)} fusion(f32[10,256,256]{2,1,0:T(8,128)S(1)} %copy-done.2, f32[1,1,4,10,256,256]{5,4,3,2,1,0:T(8,128)} %param.4, f32[1,1,1,256,256]{3,4,2,1,0:T(8,128)S(1)} %copy-done.6), kind=kOutput, calls=%fused_computation.35 | convolution fusion | flops 2013396992 | bytes 5767168 | tf_op jit(solution)/shard_map/kab,kbc->ac/dot_general | solution.py:39
  195.4 1.7 convolution_bitcast_fusion.1
  197.2 18.0 %reduce-scatter.2.cloned.1.call-done = f32[64,256]{1,0:T(8,128)} async-done(((f32[256,256]{1,0:T(8,128)}), f32[64,256]{1,0:T(8,128)}) %reduce-scatter.2.cloned.1.call-update) | async-done | bytes 65552 | tf_op jit(solution)/shard_map/reduce_scatter | solution.py:47
  215.2 10.1 %all-gather = f32[512,256]{1,0:T(8,128)S(1)} all-gather(f32[64,256]{1,0:T(8,128)} %reduce-scatter.2.cloned.1.call-done), channel_id=2, replica_groups=mesh['gx'=4,'gy'=2,'gz'=4] {'gx','gy'}, dimensions={0}, use_global_device_ids=true | all-gather | bytes 589824 | tf_op jit(solution)/shard_map/all_gather | solution.py:48
  225.3 14.7 %all_gather.11 = f32[256,256]{1,0:T(8,128)S(1)} all-gather(f32[64,256]{1,0:T(8,128)S(1)} %reduce_sum.9), channel_id=1, replica_groups=mesh['gx'=4,'gy'=2,'gz'=4] {'gz'}, dimensions={0}, use_global_device_ids=true | all-gather | bytes 327680 | tf_op jit(solution)/shard_map/all_gather | solution.py:49
  240.4 11.7 %cholesky.50 = f32[128,128]{1,0:T(8,128)S(1)} custom-call(f32[128,128]{1,0:T(8,128)S(1)} %cholesky.118), custom_call_target="Cholesky" | custom-call | tf_op jit(solution)/shard_map/jit(cholesky)/cholesky | solution.py:51
  252.2 9.8 %custom-call.14 = f32[1,128,128]{1,2,0:T(8,128)S(1)} custom-call(f32[1,128,128]{2,1,0:T(8,128)S(1)} %get-tuple-element.35), custom_call_target="InvertDiagBlocksLowerTriangular" | custom-call | tf_op jit(solution)/shard_map/jit(cholesky)/cholesky | solution.py:51
  262.5 11.7 %cholesky.105 = f32[128,128]{1,0:T(8,128)S(1)} custom-call(f32[128,128]{1,0:T(8,128)S(1)} %convolution_subtract_fusion.1), custom_call_target="Cholesky" | custom-call | tf_op jit(solution)/shard_map/jit(cholesky)/cholesky | solution.py:51
  276.3 4.2 %while.1 = (s32[]{:T(128)}, f32[256,256]{1,0:T(8,128)S(1)}, s32[2,2]{1,0:T(2,128)S(1)}, f32[2,128,128]{2,1,0:T(8,128)S(1)}, s32[]{:T(128)}) while((s32[]{:T(128)}, f32[256,256]{1,0:T(8,128)S(1)}, s32[2,2]{1,0:T(2,128)S(1)}, f32[2,128,128]{2,1,0:T(8,128)S(1)}, s32[]{:T(128)}) %tuple.37), condition=%wide.while_cond, body=%wide.while_body.sunk | while | flops 2 | bytes 131181 | solution.py:52
  277.1 1.4 bitcast_dynamic-update-slice_fusion.2
  280.5 19.7 %custom-call.15 = f32[2,128,128]{1,2,0:T(8,128)S(1)} custom-call(f32[2,128,128]{2,1,0:T(8,128)S(1)} %get-tuple-element.9), custom_call_target="InvertDiagBlocksLowerTriangular" | custom-call | tf_op jit(solution)/shard_map/triangular_solve | solution.py:52
  301.0 2.8 convolution_bitcast_fusion
  (56 shorter events, 13.2 us)
Async XLA Ops:
  7.2 208.0 %reduce-scatter.2.cloned.1.call-start = ((), (), s32[]{:S(2)}) async-start(), calls=%async_computation.1 | async-start | bytes 327680 | tf_op jit(solution)/shard_map/reduce_scatter | solution.py:47
  7.2 27.8 %copy-start.4 = (f32[1,1,4,256,256]{4,3,2,1,0:T(8,128)S(1)}, f32[1,1,4,256,256]{4,3,2,1,0:T(8,128)}, u32[]{:S(2)}) copy-start(f32[1,1,4,256,256]{4,3,2,1,0:T(8,128)} %param.3) | copy-start | bytes 3145732
  7.2 27.7 %collective-permute-start = (f32[1,1,4,256,256]{4,3,2,1,0:T(8,128)}, f32[1,1,4,256,256]{4,3,2,1,0:T(8,128)S(1)}, u32[]{:S(2)}, u32[]{:S(2)}) collective-permute-start(f32[1,1,4,256,256]{4,3,2,1,0:T(8,128)} %param.3), channel_id=1, source_target_pairs={{0,8},{8,16},{16,24},{1,9},{9,17},{17,25},{2,10},{10,18},{18,26},{... | collective-permute-start | bytes 3145736 | tf_op jit(solution)/shard_map/ppermute | solution.py:14
  12.3 47.0 %collective-permute-start.1 = (f32[1,1,4,256,256]{4,3,2,1,0:T(8,128)}, f32[1,1,4,256,256]{4,3,2,1,0:T(8,128)S(1)}, u32[]{:S(2)}, u32[]{:S(2)}) collective-permute-start(f32[1,1,4,256,256]{4,3,2,1,0:T(8,128)} %param.3), channel_id=1, source_target_pairs={{8,0},{16,8},{24,16},{9,1},{17,9},{25,17},{10,2},{18,10},{26,18},{... | collective-permute-start | bytes 3145736 | tf_op jit(solution)/shard_map/ppermute | solution.py:15
  59.3 6.6 %collective-permute-start.2 = (f32[3,1,4,256,256]{4,3,2,1,0:T(8,128)S(1)}, f32[3,1,4,256,256]{4,3,2,1,0:T(8,128)S(1)}, u32[]{:S(2)}, u32[]{:S(2)}) collective-permute-start(f32[3,1,4,256,256]{4,3,2,1,0:T(8,128)S(1)} %constant_dynamic-update-slice_fusion), channel_id=1, source_target_pairs={{0,4},{1,5},{2,6},{3,7},{8,12},{9,13},{10,14},{11,15},{16,20},{17,... | collective-permute-start | bytes 9437192 | tf_op jit(solution)/shard_map/ppermute | solution.py:14
  60.8 7.6 %collective-permute-start.3 = (f32[3,1,4,256,256]{4,3,2,1,0:T(8,128)S(1)}, f32[3,1,4,256,256]{4,3,2,1,0:T(8,128)S(1)}, u32[]{:S(2)}, u32[]{:S(2)}) collective-permute-start(f32[3,1,4,256,256]{4,3,2,1,0:T(8,128)S(1)} %constant_dynamic-update-slice_fusion), channel_id=1, source_target_pairs={{4,0},{5,1},{6,2},{7,3},{12,8},{13,9},{14,10},{15,11},{20,16},{21,... | collective-permute-start | bytes 9437192 | tf_op jit(solution)/shard_map/ppermute | solution.py:15
  65.9 5.3 %copy-start = (f32[3,1,4,256,256]{4,3,2,1,0:T(8,128)}, f32[3,1,4,256,256]{4,3,2,1,0:T(8,128)S(1)}, u32[]{:S(2)}) copy-start(f32[3,1,4,256,256]{4,3,2,1,0:T(8,128)S(1)} %collective-permute-done.2) | copy-start | bytes 9437188
  68.4 3.0 copy-start.1
  71.4 12.8 %copy-start.8 = (s32[1,1,4,10]{3,2,1,0:T(4,128)S(1)}, s32[1,1,4,10]{3,2,1,0:T(4,128)}, u32[]{:S(2)}) copy-start(s32[1,1,4,10]{3,2,1,0:T(4,128)} %param.5) | copy-start | bytes 484
  71.4 54.7 %collective-permute-start.4 = (f32[3,3,1,256,256]{4,3,2,1,0:T(8,128)}, f32[3,3,1,256,256]{4,3,2,1,0:T(8,128)}, u32[]{:S(2)}, u32[]{:S(2)}) collective-permute-start(f32[3,3,1,256,256]{4,3,2,1,0:T(8,128)} %get-tuple-element.24), channel_id=1, source_target_pairs={{0,1},{1,2},{2,3},{4,5},{5,6},{6,7},{8,9},{9,10},{10,11},{12,13},{... | collective-permute-start | bytes 7077896 | tf_op jit(solution)/shard_map/ppermute | solution.py:14
  76.5 55.2 %collective-permute-start.5 = (f32[3,3,1,256,256]{4,3,2,1,0:T(8,128)}, f32[3,3,1,256,256]{4,3,2,1,0:T(8,128)}, u32[]{:S(2)}, u32[]{:S(2)}) collective-permute-start(f32[3,3,1,256,256]{4,3,2,1,0:T(8,128)} %get-tuple-element.25), channel_id=1, source_target_pairs={{1,0},{2,1},{3,2},{5,4},{6,5},{7,6},{9,8},{10,9},{11,10},{13,12},{... | collective-permute-start | bytes 7077896 | tf_op jit(solution)/shard_map/ppermute | solution.py:15
  161.8 7.4 %copy-start.7 = (f32[1,1,1,256,256]{3,4,2,1,0:T(8,128)S(1)}, f32[1,1,1,256,256]{3,4,2,1,0:T(8,128)}, u32[]{:S(2)}) copy-start(f32[1,1,1,256,256]{3,4,2,1,0:T(8,128)} %copy.39) | copy-start | bytes 786436
  169.2 7.0 %copy-start.3 = (f32[10,256,256]{2,1,0:T(8,128)S(1)}, f32[10,256,256]{2,1,0:T(8,128)}, u32[]{:S(2)}) copy-start(f32[10,256,256]{2,1,0:T(8,128)} %gather_fusion.2) | copy-start | bytes 7864324
  176.2 6.3 %copy-start.5 = (f32[1,1,1,256,256]{3,4,2,1,0:T(8,128)S(1)}, f32[1,1,1,256,256]{3,4,2,1,0:T(8,128)}, u32[]{:S(2)}) copy-start(f32[1,1,1,256,256]{3,4,2,1,0:T(8,128)} %copy.37) | copy-start | bytes 786436
  182.5 6.7 %copy-start.2 = (f32[10,256,256]{2,1,0:T(8,128)S(1)}, f32[10,256,256]{2,1,0:T(8,128)}, u32[]{:S(2)}) copy-start(f32[10,256,256]{2,1,0:T(8,128)} %gather_fusion) | copy-start | bytes 7864324
  182.5 6.7 %copy-start.6 = (f32[1,1,1,256,256]{3,4,2,1,0:T(8,128)S(1)}, f32[1,1,1,256,256]{3,4,2,1,0:T(8,128)}, u32[]{:S(2)}) copy-start(f32[1,1,1,256,256]{3,4,2,1,0:T(8,128)} %copy.36) | copy-start | bytes 786436
Sparse Core Ops, SparseCore 0:
  197.3 17.8 reduce-scatter.1
